TPU v7x, 32 devices: a whole 2x2x4 slice. The times are simulated.
32 devices in a mesh: pair: 8 (over z, x), row: 4 (over y, core).
Axes of the slice: x: 2, y: 2, z: 4, core: 2. Of those that a mesh axis runs over, the one named last changes fastest.
Arguments:
- records: bfloat16 [128, 4096, 8], P('row', 'pair'), may hold values from -10 to 10
- offsets: float32 [8, 128], P('pair', 'row'), may hold values from -1 to 1
- counts: int32 [8], replicated, may hold values from 64 to 128, as said below
- damping: float32 [1], replicated, may hold values from 0.1 to 1
Outputs:
- offset_step: float32 [8, 128], P('pair', 'row')
Inputs may be any that keep to these rules, and one draw needn't show every extreme that they name: Channel i of block b is live when i < counts[b]; in every draw some block has all 128 channels live.
All inputs are finite; a program needn't handle non-finite values.
Results may differ from a plain program's by a relative error of at most 0.0044.
Values may be sent and summed in bfloat16 or wider, within the bound.
No kernel may reach another device: no remote copies, remote signals or barrier semaphores. Data moves between devices by JAX's collectives and lax.ppermute only.
A program may use at most 64 MiB of HBM per device.

v0:
```python
import math
import jax
import jax.numpy as jnp
from jax import lax
from jax.sharding import PartitionSpec as P

CB = 128
NF = 512
NLAG = 256


def band_table(row_start, row_count, samples, first_bin, freq_count):
    sample_ids = row_start + jnp.arange(row_count, dtype=jnp.int32)
    freq_bins = first_bin + jnp.arange(freq_count, dtype=jnp.int32)
    phase_ids = sample_ids[:, None] * freq_bins[None, :] % samples
    angles = phase_ids.astype(jnp.float32) * (2.0 * math.pi / samples)
    return jnp.concatenate([jnp.cos(angles), jnp.sin(angles)], axis=1)


def lag_weights(samples, first_bin, freq_count, lag_count):
    freq_bins = first_bin + jnp.arange(freq_count, dtype=jnp.int32)
    lag_ids = 1 + jnp.arange(lag_count, dtype=jnp.int32)
    phase_ids = freq_bins[:, None] * lag_ids[None, :] % samples
    angles = phase_ids.astype(jnp.float32) * (2.0 * math.pi / samples)
    centre = (jnp.arange(freq_count, dtype=jnp.float32) + 0.5) * (math.pi / freq_count)
    weight = jnp.sin(centre) ** 2
    return (-2.0 * weight[:, None] * jnp.sin(angles)).astype(jnp.bfloat16)


def pair_stats(own_spec, partners, lag_table, angular):
    own_re = own_spec[:, 0].astype(jnp.float32)
    own_im = own_spec[:, 1].astype(jnp.float32)
    far_re = partners[:, :, 0].astype(jnp.float32)
    far_im = partners[:, :, 1].astype(jnp.float32)
    cross_re = own_re * far_re + own_im * far_im
    cross_im = own_im * far_re - own_re * far_im
    stacked = jnp.stack([cross_im, angular * cross_re]).astype(jnp.bfloat16)
    lagged = jnp.dot(stacked, lag_table, preferred_element_type=jnp.float32)
    residual = lagged[0]
    jacobian = lagged[1]
    return (jnp.sum(jacobian * jacobian, axis=-1), jnp.sum(jacobian * residual, axis=-1))


def per_device(records, offsets, counts, damping):
    nblock = lax.axis_size("pair")
    block_rank = lax.axis_index("pair")
    quarter = lax.axis_index("row")
    relaid = lax.all_to_all(records, "pair", split_axis=2, concat_axis=1, tiled=True)
    signal = relaid[:, :, 0]
    channels = signal.shape[0]
    samples = signal.shape[1]
    first_bin = samples // 8
    block_len = samples // 8

    def accumulate(partial_value, turn_index):
        first_row = turn_index * block_len
        segment = lax.dynamic_slice_in_dim(signal, first_row, block_len, 1)
        dft_table = band_table(first_row, block_len, samples, first_bin, NF)
        table_high = dft_table.astype(jnp.bfloat16)
        table_low = (dft_table - table_high.astype(jnp.float32)).astype(jnp.bfloat16)
        partial_value = partial_value + jnp.dot(
            segment, table_high, preferred_element_type=jnp.float32
        )
        partial_value = partial_value + jnp.dot(
            segment, table_low, preferred_element_type=jnp.float32
        )
        return (partial_value, None)

    spectrum, _ = lax.scan(
        accumulate, jnp.zeros((channels, 2 * NF), jnp.float32), jnp.arange(8, dtype=jnp.int32)
    )
    cosine_part = spectrum[:, :NF]
    sine_part = spectrum[:, NF:]
    angular = (first_bin + jnp.arange(NF, dtype=jnp.int32)).astype(jnp.float32) * (
        2.0 * math.pi / samples
    )
    shift_angle = offsets[0][:, None] * angular[None, :]
    shift_cos = jnp.cos(shift_angle)
    shift_sin = jnp.sin(shift_angle)
    real_part = cosine_part * shift_cos + sine_part * shift_sin
    imag_part = cosine_part * shift_sin - sine_part * shift_cos
    live_count = lax.dynamic_index_in_dim(counts, block_rank, keepdims=False)
    channel_ids = quarter * channels + jnp.arange(channels, dtype=jnp.int32)
    alive = (channel_ids < live_count).astype(jnp.float32)
    energy = jnp.mean(real_part * real_part + imag_part * imag_part, axis=1)
    weight_scale = alive / jnp.sqrt(energy + 1e-06)
    own_spec = jnp.stack(
        [real_part * weight_scale[:, None], imag_part * weight_scale[:, None]], axis=1
    ).astype(jnp.bfloat16)
    lag_table = lag_weights(samples, first_bin, NF, NLAG)
    segment = lax.all_gather(own_spec[None], "pair", axis=0, tiled=True)
    squares_part, products_part = pair_stats(own_spec, segment, lag_table, angular)
    partner_ids = jnp.arange(segment.shape[0], dtype=jnp.int32)
    keep_mask = (partner_ids > block_rank).astype(jnp.float32)[:, None]
    new_squares = squares_part * keep_mask
    new_products = products_part * keep_mask
    eye_blocks = jnp.eye(nblock, dtype=jnp.float32)
    onehot = (jnp.arange(nblock, dtype=jnp.int32) == block_rank).astype(jnp.float32)
    sq_t = new_squares.T
    pr_t = new_products.T
    crossing = sq_t[:, None, :] * onehot[None, :, None]
    diag_vals = sq_t + onehot[None, :] * jnp.sum(sq_t, axis=1, keepdims=True)
    hessian = diag_vals[:, :, None] * eye_blocks[None] - crossing - jnp.swapaxes(crossing, 1, 2)
    gradient = onehot[None, :] * jnp.sum(pr_t, axis=1, keepdims=True) - pr_t
    hessian, gradient = lax.psum((hessian, gradient), "pair")
    diagonal = jnp.diagonal(hessian, axis1=1, axis2=2)
    trace_sum = lax.psum(jnp.sum(diagonal), "row")
    level_mean = trace_sum / (nblock * CB)
    damped = damping[0] * (diagonal + level_mean)
    system = hessian + damped[:, :, None] * eye_blocks[None]
    factor = jnp.linalg.cholesky(system)
    update = -jax.scipy.linalg.cho_solve((factor, True), gradient[:, :, None])[:, :, 0]
    return lax.dynamic_slice_in_dim(update, block_rank, 1, 1).T


def solution(mesh):
    return jax.shard_map(
        per_device,
        mesh=mesh,
        in_specs=(P("row", "pair", None), P("pair", "row"), P(), P()),
        out_specs=P("pair", "row"),
        check_vma=False,
    )
```

profile of v0, /device:TPU:0, one launch (start us, length us, event | category | flops | bytes accessed | tf_op | source)
XLA Modules:
  0.0 172.0 jit_solution(3710374380044799579)
XLA Ops:
  0.0 1.7 %copy.35 = bf16[32,512,8]{1,0,2:T(8,128)(2,1)} copy(bf16[32,512,8]{1,2,0:T(8,128)(2,1)} %param.6) | data formatting | bytes 524288 | tf_op args[0]
  1.7 7.3 %all-to-all-start = ((bf16[32,512,8]{1,0,2:T(8,128)(2,1)}), bf16[32,512,8]{1,0,2:T(8,128)(2,1)S(1)}, u32[]{:S(2)}, u32[]{:S(2)}) async-start(bf16[32,512,8]{1,0,2:T(8,128)(2,1)} %copy.35), calls=%async_computation | async-start | bytes 524288 | tf_op jit(solution)/shard_map/all_to_all | solution.py:48
  9.2 0.6 dynamic_slice.20
  9.9 8.1 %all-to-all-done = bf16[32,512,8]{1,0,2:T(8,128)(2,1)S(1)} async-done(((bf16[32,512,8]{1,0,2:T(8,128)(2,1)}), bf16[32,512,8]{1,0,2:T(8,128)(2,1)S(1)}, u32[]{:S(2)}, u32[]{:S(2)}) %all-to-all-start) | async-done | bytes 262176 | tf_op jit(solution)/shard_map/all_to_all | solution.py:48
  18.0 48.9 %while.13 = (s32[]{:T(128)}, f32[32,1024]{1,0:T(8,128)S(1)}, s32[8]{0:T(128)S(1)}, bf16[32,4096]{1,0:T(8,128)(2,1)S(1)}, s32[]{:T(128)}, /*index=5*/s32[1]{0:T(128)}, s32[]{:T(128)}, s32[]{:T(128)}) while((s32[]{:T(128)}, f32[32,1024]{1,0:T(8,128)S(1)}, s32[8]{0:T(128)S(1)}, bf16[32,4096]{1,0:T(8,128)(2,1)S(1)}, s32[]{:T(128)}, ...), condition=%wide.region_1.2_spmd.clone, body=%wide.region_0.1_spmd.clone.sunk | while | flops 75596808 | bytes 6889645 | solution.py:69
  18.0 0.7 dynamic_slice.34
  19.4 4.1 %fusion.70 = (f32[512,512]{1,0:T(8,128)S(1)}, f32[512,512]{1,0:T(8,128)S(1)}) fusion(s32[512]{0:T(512)S(1)} %get-tuple-element.138, s32[512]{0:T(512)S(1)} %get-tuple-element.139), kind=kLoop, calls=%fused_computation.16.clone.1 | loop fusion | flops 3670016 | bytes 2101248 | tf_op jit(solution)/shard_map/while/body/eval_jaxpr/cos | solution.py:17
  23.5 0.3 fusion.71
  23.8 0.3 convolution_add_fusion.2
  24.1 0.7 dynamic_slice.34
  25.5 4.1 %fusion.70 = (f32[512,512]{1,0:T(8,128)S(1)}, f32[512,512]{1,0:T(8,128)S(1)}) fusion(s32[512]{0:T(512)S(1)} %get-tuple-element.138, s32[512]{0:T(512)S(1)} %get-tuple-element.139), kind=kLoop, calls=%fused_computation.16.clone.1 | loop fusion | flops 3670016 | bytes 2101248 | tf_op jit(solution)/shard_map/while/body/eval_jaxpr/cos | solution.py:17
  29.6 0.3 fusion.71
  29.9 0.3 convolution_add_fusion.2
  30.2 0.7 dynamic_slice.34
  31.6 4.1 %fusion.70 = (f32[512,512]{1,0:T(8,128)S(1)}, f32[512,512]{1,0:T(8,128)S(1)}) fusion(s32[512]{0:T(512)S(1)} %get-tuple-element.138, s32[512]{0:T(512)S(1)} %get-tuple-element.139), kind=kLoop, calls=%fused_computation.16.clone.1 | loop fusion | flops 3670016 | bytes 2101248 | tf_op jit(solution)/shard_map/while/body/eval_jaxpr/cos | solution.py:17
  35.8 0.3 fusion.71
  36.1 0.3 convolution_add_fusion.2
  36.3 0.7 dynamic_slice.34
  37.7 4.1 %fusion.70 = (f32[512,512]{1,0:T(8,128)S(1)}, f32[512,512]{1,0:T(8,128)S(1)}) fusion(s32[512]{0:T(512)S(1)} %get-tuple-element.138, s32[512]{0:T(512)S(1)} %get-tuple-element.139), kind=kLoop, calls=%fused_computation.16.clone.1 | loop fusion | flops 3670016 | bytes 2101248 | tf_op jit(solution)/shard_map/while/body/eval_jaxpr/cos | solution.py:17
  41.9 0.3 fusion.71
  42.2 0.3 convolution_add_fusion.2
  42.5 0.7 dynamic_slice.34
  43.8 4.1 %fusion.70 = (f32[512,512]{1,0:T(8,128)S(1)}, f32[512,512]{1,0:T(8,128)S(1)}) fusion(s32[512]{0:T(512)S(1)} %get-tuple-element.138, s32[512]{0:T(512)S(1)} %get-tuple-element.139), kind=kLoop, calls=%fused_computation.16.clone.1 | loop fusion | flops 3670016 | bytes 2101248 | tf_op jit(solution)/shard_map/while/body/eval_jaxpr/cos | solution.py:17
  48.0 0.3 fusion.71
  48.3 0.3 convolution_add_fusion.2
  48.6 0.7 dynamic_slice.34
  50.0 4.1 %fusion.70 = (f32[512,512]{1,0:T(8,128)S(1)}, f32[512,512]{1,0:T(8,128)S(1)}) fusion(s32[512]{0:T(512)S(1)} %get-tuple-element.138, s32[512]{0:T(512)S(1)} %get-tuple-element.139), kind=kLoop, calls=%fused_computation.16.clone.1 | loop fusion | flops 3670016 | bytes 2101248 | tf_op jit(solution)/shard_map/while/body/eval_jaxpr/cos | solution.py:17
  54.1 0.3 fusion.71
  54.4 0.3 convolution_add_fusion.2
  54.7 0.7 dynamic_slice.34
  56.1 4.1 %fusion.70 = (f32[512,512]{1,0:T(8,128)S(1)}, f32[512,512]{1,0:T(8,128)S(1)}) fusion(s32[512]{0:T(512)S(1)} %get-tuple-element.138, s32[512]{0:T(512)S(1)} %get-tuple-element.139), kind=kLoop, calls=%fused_computation.16.clone.1 | loop fusion | flops 3670016 | bytes 2101248 | tf_op jit(solution)/shard_map/while/body/eval_jaxpr/cos | solution.py:17
  60.2 0.3 fusion.71
  60.5 0.3 convolution_add_fusion.2
  60.8 0.7 dynamic_slice.34
  62.2 4.1 %fusion.70 = (f32[512,512]{1,0:T(8,128)S(1)}, f32[512,512]{1,0:T(8,128)S(1)}) fusion(s32[512]{0:T(512)S(1)} %get-tuple-element.138, s32[512]{0:T(512)S(1)} %get-tuple-element.139), kind=kLoop, calls=%fused_computation.16.clone.1 | loop fusion | flops 3670016 | bytes 2101248 | tf_op jit(solution)/shard_map/while/body/eval_jaxpr/cos | solution.py:17
  66.4 0.3 fusion.71
  66.6 0.3 convolution_add_fusion.2
  66.9 0.4 add_reduce_fusion
  67.4 0.6 compare_select_fusion
  68.1 31.6 %all_gather.3 = bf16[8,32,2,512]{3,1,0,2:T(8,128)(2,1)S(1)} all-gather(bf16[1,32,2,512]{3,1,0,2:T(8,128)(2,1)S(1)} %pad_maximum_fusion.1), channel_id=1, replica_groups=mesh['pair'=8,'row'=4] {'pair'}, dimensions={0}, use_global_device_ids=true | all-gather | bytes 589824 | tf_op jit(solution)/shard_map/all_gather | solution.py:91
  99.9 2.3 %fusion.28 = f32[2,8,32,256]{3,2,1,0:T(8,128)S(1)} fusion(bf16[1,8,32,512]{3,2,1,0:T(8,128)(2,1)S(1)} %get-tuple-element.99, bf16[1,8,32,512]{3,2,1,0:T(8,128)(2,1)S(1)} %get-tuple-element.98, s32[256]{0:T(256)S(1)} %iota_add_fusion.3, s32[512]{0:T(512)S(1)} %iota_add_fusion.2, f32[512]{0:T(512)S(1)} %multiply_multiply_fusion), kind=kOutput, calls=%fused_computation.45 | convolution fusion | flops 136577024 | bytes 1053696 | tf_op jit(solution)/shard_map/dot_general | solution.py:38
  102.6 35.2 %all-reduce = (f32[32,8,8]{0,1,2:T(8,128)S(1)}, f32[32,8]{0,1:T(8,128)S(1)}) all-reduce(f32[32,8,8]{0,1,2:T(8,128)S(1)} %multiply_subtract_fusion, f32[32,8]{0,1:T(8,128)S(1)} %get-tuple-element.104), channel_id=1, replica_groups=mesh['pair'=8,'row'=4] {'pair'}, use_global_device_ids=true, to_apply=%region_5.6 | all-reduce | flops 2304 | bytes 18432 | tf_op jit(solution)/shard_map/psum | solution.py:105
  137.8 0.6 gather_fusion
  138.4 0.7 reduce_sum.57
  139.7 6.3 %psum.22 = f32[]{:T(128)} all-reduce(f32[]{:T(128)} %reduce_sum.57), channel_id=1, replica_groups=mesh['pair'=8,'row'=4] {'row'}, use_global_device_ids=true, to_apply=%region_7.8 | all-reduce | flops 1 | bytes 8 | tf_op jit(solution)/shard_map/psum | solution.py:107
  146.9 23.5 %custom-call.11 = f32[32,8,8]{2,1,0:T(8,128)S(1)} custom-call(f32[32,8,8]{2,1,0:T(8,128)S(1)} %broadcast_multiply_fusion), custom_call_target="Cholesky" | custom-call | tf_op jit(solution)/shard_map/jit(cholesky)/cholesky | solution.py:111
  170.7 0.7 custom-call.12
  171.5 0.5 dynamic-slice_bitcast_fusion
  (45 shorter events, 1.5 us)
Async XLA Ops:
  0.0 9.2 %copy-start.1 = (s32[8]{0:T(128)S(1)}, s32[8]{0:T(128)}, u32[]{:S(2)}) copy-start(s32[8]{0:T(128)} %param.8) | copy-start | bytes 100
  1.7 16.2 %all-to-all-start = ((bf16[32,512,8]{1,0,2:T(8,128)(2,1)}), bf16[32,512,8]{1,0,2:T(8,128)(2,1)S(1)}, u32[]{:S(2)}, u32[]{:S(2)}) async-start(bf16[32,512,8]{1,0,2:T(8,128)(2,1)} %copy.35), calls=%async_computation | async-start | bytes 524288 | tf_op jit(solution)/shard_map/all_to_all | solution.py:48
  18.0 49.0 %copy-start = (f32[1,32]{1,0:T(1,128)S(1)}, f32[1,32]{1,0:T(1,128)}, u32[]{:S(2)}) copy-start(f32[1,32]{1,0:T(1,128)} %param.7) | copy-start | bytes 388
where the time goes:
time: 172 us
  blocking collectives  73.1 us (42%)
  other arithmetic  60.2 us (35%)
  local copies, waits for them, and re-layouts  9.21 us (5%)
  waiting for transfers between devices  8.06 us (5%)
  starting transfers between devices  7.28 us (4%)
  matrix products  6.83 us (4%)
  loops' own time  5.79 us (3%)
    psum x1, blocking collectives, per_device(): hessian, gradient = lax.psum((hessian, gradient), 'pair')  35.2 us
    cos x8, other arithmetic, band_table(): return jnp.concatenate([jnp.cos(angles), jnp.sin(angles)], axis=1)  33.2 us
    all_gather x1, blocking collectives, per_device(): segment = lax.all_gather(own_spec[None], 'pair', axis=0, tiled=True)  31.6 us
    another operation x4, other arithmetic, per_device(): factor = jnp.linalg.cholesky(system)  23.6 us
    all_to_all x1, waiting for transfers between devices, per_device(): lax.all_to_all(records, 'pair', split_axis=2, concat_axis=1, tiled=True)  8.06 us
    all_to_all x1, starting transfers between devices, per_device(): lax.all_to_all(records, 'pair', split_axis=2, concat_axis=1, tiled=True)  7.28 us
    psum x1, blocking collectives, per_device(): trace_sum = lax.psum(jnp.sum(diagonal), 'row')  6.25 us
    another operation x1, loops' own time, per_device(): lax.scan(accumulate, jnp.zeros((channels, 2 * NF), jnp.float32), jnp.aran...  5.79 us
  transfers between devices with their start and end apart: 1, of which 1 were waited for; matrix products, arithmetic and copies ran while one was open for 0% of the time, Pallas kernels for 0%

commit v1 on v0

--- a/solution.py
+++ b/solution.py
@@ -7,6 +7,14 @@
 CB = 128
 NF = 512
 NLAG = 256
+
+
+def tiled_gather(value, axis, dim):
+    size = lax.axis_size(axis)
+    repeats = [size if d == dim else 1 for d in range(value.ndim)]
+    return lax.all_to_all(
+        jnp.tile(value, repeats), axis, split_axis=dim, concat_axis=dim, tiled=True
+    )
 
 
 def band_table(row_start, row_count, samples, first_bin, freq_count):
@@ -88,7 +96,7 @@
         [real_part * weight_scale[:, None], imag_part * weight_scale[:, None]], axis=1
     ).astype(jnp.bfloat16)
     lag_table = lag_weights(samples, first_bin, NF, NLAG)
-    segment = lax.all_gather(own_spec[None], "pair", axis=0, tiled=True)
+    segment = tiled_gather(own_spec[None], "pair", 0)
     squares_part, products_part = pair_stats(own_spec, segment, lag_table, angular)
     partner_ids = jnp.arange(segment.shape[0], dtype=jnp.int32)
     keep_mask = (partner_ids > block_rank).astype(jnp.float32)[:, None]

time: 172 us -> 160 us (0.930)
  blocking collectives: 73.1 us -> 41.8 us
  waiting for transfers between devices: 8.06 us -> 22.2 us
  starting transfers between devices: 7.28 us -> 10.9 us
    all_gather x1 -> x0, blocking collectives: 31.6 us -> none  [per_device(): segment = lax.all_gather(own_spec[None], 'pair', axis=0, tiled=True)]
    all_to_all x0 -> x1, waiting for transfers between devices: none -> 14 us  [tiled_gather(): lax.all_to_all(jnp.tile(value, repeats), axis, split_axis=dim, concat_axi...]
    all_to_all x0 -> x1, starting transfers between devices: none -> 3.59 us  [tiled_gather(): lax.all_to_all(jnp.tile(value, repeats), axis, split_axis=dim, concat_axi...]
  transfers between devices with their start and end apart: 1 -> 2, of which waited for: 1 -> 2; matrix products, arithmetic and copies ran while one was open for 0% -> 1% of each run, Pallas kernels for 0% -> 0%
where the time goes in v1:
time: 160 us; the launch traced here: 159 us
  other arithmetic  60.2 us (38%)
  blocking collectives  41.8 us (26%)
  waiting for transfers between devices  22.2 us (14%)
  starting transfers between devices  10.9 us (7%)
  local copies, waits for them, and re-layouts  10.1 us (6%)
  matrix products  6.83 us (4%)
  loops' own time  5.79 us (4%)
    psum x1, blocking collectives, per_device(): hessian, gradient = lax.psum((hessian, gradient), 'pair')  35.5 us
    cos x8, other arithmetic, band_table(): return jnp.concatenate([jnp.cos(angles), jnp.sin(angles)], axis=1)  33.2 us
    another operation x4, other arithmetic, per_device(): factor = jnp.linalg.cholesky(system)  23.6 us
    all_to_all x1, waiting for transfers between devices, tiled_gather(): lax.all_to_all(jnp.tile(value, repeats), axis, split_axis=dim, concat_axi...  14 us
    all_to_all x1, waiting for transfers between devices, per_device(): lax.all_to_all(records, 'pair', split_axis=2, concat_axis=1, tiled=True)  8.26 us
    all_to_all x1, starting transfers between devices, per_device(): lax.all_to_all(records, 'pair', split_axis=2, concat_axis=1, tiled=True)  7.28 us
    psum x1, blocking collectives, per_device(): trace_sum = lax.psum(jnp.sum(diagonal), 'row')  6.25 us
    another operation x1, loops' own time, per_device(): lax.scan(accumulate, jnp.zeros((channels, 2 * NF), jnp.float32), jnp.aran...  5.79 us
  transfers between devices with their start and end apart: 2, of which 2 were waited for; matrix products, arithmetic and copies ran while one was open for 1% of the time, Pallas kernels for 0%

profile of v1, /device:TPU:0, one launch (start us, length us, event | category | flops | bytes accessed | tf_op | source)
XLA Modules:
  0.0 159.3 jit_solution(7879578481115024471)
XLA Ops:
  0.0 1.7 %copy.36 = bf16[32,512,8]{1,0,2:T(8,128)(2,1)} copy(bf16[32,512,8]{1,2,0:T(8,128)(2,1)} %param.6) | data formatting | bytes 524288 | tf_op args[0]
  1.7 7.3 %all-to-all-start = ((bf16[32,512,8]{1,0,2:T(8,128)(2,1)}), bf16[32,512,8]{1,0,2:T(8,128)(2,1)S(1)}, u32[]{:S(2)}, u32[]{:S(2)}) async-start(bf16[32,512,8]{1,0,2:T(8,128)(2,1)} %copy.36), calls=%async_computation | async-start | bytes 524288 | tf_op jit(solution)/shard_map/all_to_all | solution.py:56
  9.0 0.7 dynamic_slice.20
  9.7 8.3 %all-to-all-done = bf16[32,512,8]{1,0,2:T(8,128)(2,1)S(1)} async-done(((bf16[32,512,8]{1,0,2:T(8,128)(2,1)}), bf16[32,512,8]{1,0,2:T(8,128)(2,1)S(1)}, u32[]{:S(2)}, u32[]{:S(2)}) %all-to-all-start) | async-done | bytes 262176 | tf_op jit(solution)/shard_map/all_to_all | solution.py:56
  18.0 48.9 %while.13 = (s32[]{:T(128)}, f32[32,1024]{1,0:T(8,128)S(1)}, s32[8]{0:T(128)S(1)}, bf16[32,4096]{1,0:T(8,128)(2,1)S(1)}, s32[]{:T(128)}, /*index=5*/s32[1]{0:T(128)}, s32[]{:T(128)}, s32[]{:T(128)}) while((s32[]{:T(128)}, f32[32,1024]{1,0:T(8,128)S(1)}, s32[8]{0:T(128)S(1)}, bf16[32,4096]{1,0:T(8,128)(2,1)S(1)}, s32[]{:T(128)}, ...), condition=%wide.region_1.2_spmd.clone, body=%wide.region_0.1_spmd.clone.sunk | while | flops 75596808 | bytes 6889645 | solution.py:77
  18.0 0.7 dynamic_slice.34
  19.4 4.1 %fusion.70 = (f32[512,512]{1,0:T(8,128)S(1)}, f32[512,512]{1,0:T(8,128)S(1)}) fusion(s32[512]{0:T(512)S(1)} %get-tuple-element.138, s32[512]{0:T(512)S(1)} %get-tuple-element.139), kind=kLoop, calls=%fused_computation.16.clone.1 | loop fusion | flops 3670016 | bytes 2101248 | tf_op jit(solution)/shard_map/while/body/eval_jaxpr/cos | solution.py:25
  23.5 0.3 fusion.71
  23.8 0.3 convolution_add_fusion.2
  24.1 0.7 dynamic_slice.34
  25.5 4.1 %fusion.70 = (f32[512,512]{1,0:T(8,128)S(1)}, f32[512,512]{1,0:T(8,128)S(1)}) fusion(s32[512]{0:T(512)S(1)} %get-tuple-element.138, s32[512]{0:T(512)S(1)} %get-tuple-element.139), kind=kLoop, calls=%fused_computation.16.clone.1 | loop fusion | flops 3670016 | bytes 2101248 | tf_op jit(solution)/shard_map/while/body/eval_jaxpr/cos | solution.py:25
  29.6 0.3 fusion.71
  30.2 0.7 dynamic_slice.34
  31.6 4.1 %fusion.70 = (f32[512,512]{1,0:T(8,128)S(1)}, f32[512,512]{1,0:T(8,128)S(1)}) fusion(s32[512]{0:T(512)S(1)} %get-tuple-element.138, s32[512]{0:T(512)S(1)} %get-tuple-element.139), kind=kLoop, calls=%fused_computation.16.clone.1 | loop fusion | flops 3670016 | bytes 2101248 | tf_op jit(solution)/shard_map/while/body/eval_jaxpr/cos | solution.py:25
  35.8 0.3 fusion.71
  36.1 0.3 convolution_add_fusion.2
  36.3 0.7 dynamic_slice.34
  37.7 4.1 %fusion.70 = (f32[512,512]{1,0:T(8,128)S(1)}, f32[512,512]{1,0:T(8,128)S(1)}) fusion(s32[512]{0:T(512)S(1)} %get-tuple-element.138, s32[512]{0:T(512)S(1)} %get-tuple-element.139), kind=kLoop, calls=%fused_computation.16.clone.1 | loop fusion | flops 3670016 | bytes 2101248 | tf_op jit(solution)/shard_map/while/body/eval_jaxpr/cos | solution.py:25
  41.9 0.3 fusion.71
  42.2 0.3 convolution_add_fusion.2
  42.5 0.7 dynamic_slice.34
  43.8 4.1 %fusion.70 = (f32[512,512]{1,0:T(8,128)S(1)}, f32[512,512]{1,0:T(8,128)S(1)}) fusion(s32[512]{0:T(512)S(1)} %get-tuple-element.138, s32[512]{0:T(512)S(1)} %get-tuple-element.139), kind=kLoop, calls=%fused_computation.16.clone.1 | loop fusion | flops 3670016 | bytes 2101248 | tf_op jit(solution)/shard_map/while/body/eval_jaxpr/cos | solution.py:25
  48.0 0.3 fusion.71
  48.3 0.3 convolution_add_fusion.2
  48.6 0.7 dynamic_slice.34
  50.0 4.1 %fusion.70 = (f32[512,512]{1,0:T(8,128)S(1)}, f32[512,512]{1,0:T(8,128)S(1)}) fusion(s32[512]{0:T(512)S(1)} %get-tuple-element.138, s32[512]{0:T(512)S(1)} %get-tuple-element.139), kind=kLoop, calls=%fused_computation.16.clone.1 | loop fusion | flops 3670016 | bytes 2101248 | tf_op jit(solution)/shard_map/while/body/eval_jaxpr/cos | solution.py:25
  54.1 0.3 fusion.71
  54.4 0.3 convolution_add_fusion.2
  54.7 0.7 dynamic_slice.34
  56.1 4.1 %fusion.70 = (f32[512,512]{1,0:T(8,128)S(1)}, f32[512,512]{1,0:T(8,128)S(1)}) fusion(s32[512]{0:T(512)S(1)} %get-tuple-element.138, s32[512]{0:T(512)S(1)} %get-tuple-element.139), kind=kLoop, calls=%fused_computation.16.clone.1 | loop fusion | flops 3670016 | bytes 2101248 | tf_op jit(solution)/shard_map/while/body/eval_jaxpr/cos | solution.py:25
  60.2 0.3 fusion.71
  60.8 0.7 dynamic_slice.34
  62.2 4.1 %fusion.70 = (f32[512,512]{1,0:T(8,128)S(1)}, f32[512,512]{1,0:T(8,128)S(1)}) fusion(s32[512]{0:T(512)S(1)} %get-tuple-element.138, s32[512]{0:T(512)S(1)} %get-tuple-element.139), kind=kLoop, calls=%fused_computation.16.clone.1 | loop fusion | flops 3670016 | bytes 2101248 | tf_op jit(solution)/shard_map/while/body/eval_jaxpr/cos | solution.py:25
  66.4 0.3 fusion.71
  66.6 0.3 convolution_add_fusion.2
  66.9 0.4 add_reduce_fusion
  67.4 0.6 compare_select_fusion
  68.1 0.8 tile.2
  69.0 3.6 %all-to-all-start.1 = ((bf16[8,32,2,512]{3,1,2,0:T(8,128)(2,1)}), bf16[8,32,2,512]{3,1,2,0:T(8,128)(2,1)S(1)}, u32[]{:S(2)}, u32[]{:S(2)}) async-start(bf16[8,32,2,512]{3,1,2,0:T(8,128)(2,1)} %tile.2), calls=%async_computation.1 | async-start | bytes 1048576 | tf_op jit(solution)/shard_map/all_to_all | solution.py:15
  72.7 14.0 %all-to-all-done.1 = bf16[8,32,2,512]{3,1,2,0:T(8,128)(2,1)S(1)} async-done(((bf16[8,32,2,512]{3,1,2,0:T(8,128)(2,1)}), bf16[8,32,2,512]{3,1,2,0:T(8,128)(2,1)S(1)}, u32[]{:S(2)}, u32[]{:S(2)}) %all-to-all-start.1) | async-done | bytes 524320 | tf_op jit(solution)/shard_map/all_to_all | solution.py:15
  86.9 2.3 %fusion.28 = f32[2,8,32,256]{3,2,1,0:T(8,128)S(1)} fusion(bf16[1,8,32,512]{3,2,1,0:T(8,128)(2,1)S(1)} %get-tuple-element.99, bf16[1,8,32,512]{3,2,1,0:T(8,128)(2,1)S(1)} %get-tuple-element.98, s32[256]{0:T(256)S(1)} %iota_add_fusion.3, s32[512]{0:T(512)S(1)} %iota_add_fusion.2, f32[512]{0:T(512)S(1)} %multiply_multiply_fusion), kind=kOutput, calls=%fused_computation.45 | convolution fusion | flops 136577024 | bytes 1053696 | tf_op jit(solution)/shard_map/dot_general | solution.py:46
  89.6 35.5 %all-reduce = (f32[32,8,8]{0,1,2:T(8,128)S(1)}, f32[32,8]{0,1:T(8,128)S(1)}) all-reduce(f32[32,8,8]{0,1,2:T(8,128)S(1)} %multiply_subtract_fusion, f32[32,8]{0,1:T(8,128)S(1)} %get-tuple-element.104), channel_id=1, replica_groups=mesh['pair'=8,'row'=4] {'pair'}, use_global_device_ids=true, to_apply=%region_5.6 | all-reduce | flops 2304 | bytes 18432 | tf_op jit(solution)/shard_map/psum | solution.py:113
  125.1 0.6 gather_fusion
  125.7 0.7 reduce_sum.57
  127.1 6.3 %psum.22 = f32[]{:T(128)} all-reduce(f32[]{:T(128)} %reduce_sum.57), channel_id=1, replica_groups=mesh['pair'=8,'row'=4] {'row'}, use_global_device_ids=true, to_apply=%region_7.8 | all-reduce | flops 1 | bytes 8 | tf_op jit(solution)/shard_map/psum | solution.py:115
  134.2 23.5 %custom-call.11 = f32[32,8,8]{2,1,0:T(8,128)S(1)} custom-call(f32[32,8,8]{2,1,0:T(8,128)S(1)} %broadcast_multiply_fusion), custom_call_target="Cholesky" | custom-call | tf_op jit(solution)/shard_map/jit(cholesky)/cholesky | solution.py:119
  158.1 0.7 custom-call.12
  158.8 0.5 dynamic-slice_bitcast_fusion
  (47 shorter events, 2.0 us)
Async XLA Ops:
  0.0 9.0 %copy-start.1 = (s32[8]{0:T(128)S(1)}, s32[8]{0:T(128)}, u32[]{:S(2)}) copy-start(s32[8]{0:T(128)} %param.8) | copy-start | bytes 100
  1.7 16.2 %all-to-all-start = ((bf16[32,512,8]{1,0,2:T(8,128)(2,1)}), bf16[32,512,8]{1,0,2:T(8,128)(2,1)S(1)}, u32[]{:S(2)}, u32[]{:S(2)}) async-start(bf16[32,512,8]{1,0,2:T(8,128)(2,1)} %copy.36), calls=%async_computation | async-start | bytes 524288 | tf_op jit(solution)/shard_map/all_to_all | solution.py:56
  18.0 49.0 %copy-start = (f32[1,32]{1,0:T(1,128)S(1)}, f32[1,32]{1,0:T(1,128)}, u32[]{:S(2)}) copy-start(f32[1,32]{1,0:T(1,128)} %param.7) | copy-start | bytes 388
  69.0 17.8 %all-to-all-start.1 = ((bf16[8,32,2,512]{3,1,2,0:T(8,128)(2,1)}), bf16[8,32,2,512]{3,1,2,0:T(8,128)(2,1)S(1)}, u32[]{:S(2)}, u32[]{:S(2)}) async-start(bf16[8,32,2,512]{3,1,2,0:T(8,128)(2,1)} %tile.2), calls=%async_computation.1 | async-start | bytes 1048576 | tf_op jit(solution)/shard_map/all_to_all | solution.py:15
